TPU v7x, 32 devices: a whole 2x2x4 slice. The times are simulated.
32 devices in a mesh: sx: 8 (over z, x), sy: 4 (over y, core).
Axes of the slice: x: 2, y: 2, z: 4, core: 2. Of those that a mesh axis runs over, the one named last changes fastest.
Arguments:
- activations: bfloat16 [16384, 1024], P(('sx', 'sy')), may hold values from -6 to 6
- norm_gain: float32 [1024], replicated, may hold values from 0.5 to 8
- w_local: bfloat16 [1024, 1536], replicated, may hold values from -0.1875 to 0.1875
- w_cluster: bfloat16 [1024, 3072], replicated, may hold values from -0.1875 to 0.1875
- w_output: bfloat16 [1536, 1024], replicated, may hold values from -0.15625 to 0.15625
- assignment: int32 [16384, 8], P(('sx', 'sy')), may hold values from 0 to 7, as said below
Outputs:
- layer_out: bfloat16 [16384, 1024], P(('sx', 'sy'))
Inputs may be any that keep to these rules, and one draw needn't show every extreme that they name: `assignment`: tokens d * 512 to (d + 1) * 512 - 1 form block d. In every head each cluster number is given to exactly 2048 tokens; at most 112 tokens of one block share a cluster number in one head, and in every head some block has exactly 112. Task group g of head h is the clusters g * 2 to (g + 1) * 2 - 1; at most 160 tokens of one block fall into one task group of one head, and in every head some block has exactly 160 in some group.
All inputs are finite; a program needn't handle non-finite values.
Results may differ from a plain program's by a relative error of at most 0.0035.
The roundings to bfloat16 on the way count: a program that leaves them out, or rounds other values in their place, can miss the bound.
Values may be sent and summed in bfloat16 or wider, within the bound.
A program may use at most 128 MiB of HBM per device.

v0:
```python
import jax
import jax.numpy as jnp
from jax import lax
from jax.sharding import PartitionSpec as P

HL = 4
HC = 8
HD = 128
WIN = 512
CSIZE = 2048


EPSILON = 1e-06


def shifted(value, axis, steps):
    count = lax.axis_size(axis)
    leading, last = (max(0, -steps), min(count, count - steps))
    return lax.ppermute(value, axis, [(source, source + steps) for source in range(leading, last)])


def rms_norm(activations, norm_gain):
    values = activations.astype(jnp.float32)
    mean_square = jnp.mean(values * values, axis=-1, keepdims=True)
    return (values * lax.rsqrt(mean_square + EPSILON) * norm_gain).astype(jnp.bfloat16)


def normalize_rows(scores):
    highest = jnp.max(scores, axis=-1, keepdims=True)
    raised = jnp.exp(scores - highest)
    return (raised / jnp.sum(raised, axis=-1, keepdims=True)).astype(jnp.bfloat16)


def window_attention(local_qkv, rim_rows, base_row, tok_rows):
    head_width = HL * HD
    score_scale = HD ** (-0.5)
    queries = local_qkv[:, :head_width]
    key_value = jnp.concatenate([rim_rows, local_qkv[:, head_width:]], axis=0)
    block_rows = min(512, tok_rows)

    def window_one_block(first_row):
        query_block = queries.reshape(block_rows, HL, HD)
        key_block = key_value[:, :head_width].reshape(block_rows + WIN, HL, HD)
        value_block = key_value[:, head_width:].reshape(block_rows + WIN, HL, HD)
        scores = (
            jnp.einsum("qhd,khd->hqk", query_block, key_block, preferred_element_type=jnp.float32)
            * score_scale
        )
        row_ids = jnp.arange(block_rows, dtype=jnp.int32)[:, None]
        col_ids = jnp.arange(block_rows + WIN, dtype=jnp.int32)[None, :]
        allowed = (
            (col_ids > row_ids)
            & (col_ids <= row_ids + WIN)
            & (base_row + first_row + col_ids - WIN >= 0)
        )
        scores = jnp.where(allowed[None], scores, -1e30)
        weights = normalize_rows(scores)
        mixed = jnp.einsum("hqk,khd->qhd", weights, value_block, preferred_element_type=jnp.float32)
        return mixed.astype(jnp.bfloat16).reshape(block_rows, head_width)

    starts = jnp.arange(tok_rows // block_rows, dtype=jnp.int32) * block_rows
    return lax.map(window_one_block, starts).reshape(tok_rows, head_width)


def tagged_attention(rows, query_tags, key_tags):
    score_scale = HD ** (-0.5)
    total = rows.shape[0]
    block_rows = total
    while block_rows > 512 and block_rows % 2 == 0:
        block_rows = block_rows // 2
    queries = rows[:, :HD]
    key_rows = rows[:, HD : 2 * HD]
    value_rows = rows[:, 2 * HD :]

    def tagged_one_block(first_row):
        query_block = lax.dynamic_slice_in_dim(queries, first_row, block_rows, 0)
        tag_block = lax.dynamic_slice_in_dim(query_tags, first_row, block_rows, 0)
        scores = (
            jnp.einsum("qd,kd->qk", query_block, key_rows, preferred_element_type=jnp.float32)
            * score_scale
        )
        scores = jnp.where(tag_block[:, None] == key_tags[None, :], scores, -1e30)
        weights = normalize_rows(scores)
        return jnp.dot(weights, value_rows, preferred_element_type=jnp.float32).astype(jnp.bfloat16)

    starts = jnp.arange(total // block_rows, dtype=jnp.int32) * block_rows
    return lax.map(tagged_one_block, starts).reshape(total, HD)


def pooled_tasks(pool_rows, pool_counts):
    sources, pool_size = (pool_rows.shape[0], pool_rows.shape[1])
    task_slots = pool_counts.shape[1]
    bounds = jnp.cumsum(pool_counts, axis=1)
    slot_ids = jnp.arange(pool_size, dtype=jnp.int32)
    task_of = jnp.sum(
        (bounds[:, None, :] <= slot_ids[None, :, None]).astype(jnp.int32), axis=2
    ).reshape(-1)
    alive = task_of < task_slots
    key_tags = jnp.where(alive, task_of, -1)
    result = tagged_attention(pool_rows.reshape(-1, 3 * HD), task_of, key_tags)
    result = jnp.where(alive[:, None], result, jnp.zeros_like(result))
    return result.reshape(sources, pool_size, HD)


def route_plan(assignment, cluster_count):
    tok_rows = assignment.shape[0]
    member = assignment[:, :, None] == jnp.arange(cluster_count, dtype=jnp.int32)[None, None, :]
    onehot = member.astype(jnp.bfloat16).reshape(tok_rows, HC * cluster_count)
    row_ids = jnp.arange(tok_rows, dtype=jnp.int32)
    earlier = (row_ids[:, None] > row_ids[None, :]).astype(jnp.bfloat16)
    running = jnp.dot(earlier, onehot, preferred_element_type=jnp.float32).reshape(
        tok_rows, HC, cluster_count
    )
    member_int = member.astype(jnp.int32)
    position = jnp.sum(jnp.where(member, running, 0.0), axis=2).astype(jnp.int32)
    per_task = jnp.sum(member_int, axis=0).reshape(-1)
    return (member_int, position, per_task)


def place_rows(slot_local, region, qkv_heads):
    slot_ids = jnp.arange(region, dtype=jnp.int32)
    table = (slot_ids[None, :, None] == jnp.transpose(slot_local)[:, None, :]).astype(jnp.bfloat16)
    placed = jnp.einsum(
        "hst,thf->hsf", table, qkv_heads, preferred_element_type=jnp.float32
    ).astype(jnp.bfloat16)
    return (table, placed)


def collect_rows(table, came_back, region):
    heads_back = came_back.reshape(HC, region, HD)
    mixed = jnp.einsum(
        "hst,hsf->thf", table, heads_back, preferred_element_type=jnp.float32
    ).astype(jnp.bfloat16)
    return mixed.reshape(mixed.shape[0], HC * HD)


def body(activations, norm_gain, w_local, w_cluster, w_output, assignment):
    tok_rows = activations.shape[0]
    shards = lax.axis_size(("sx", "sy"))
    mean_rows = CSIZE // shards
    task_slots = tok_rows * HC // CSIZE
    pool_size = (
        task_slots * mean_rows + mean_rows // 2 * (task_slots % 2) + task_slots * (mean_rows // 4)
    )
    cluster_count = shards * task_slots // HC
    head_width = HL * HD
    normed = rms_norm(activations, norm_gain)
    local_qkv = jnp.dot(normed, w_local, preferred_element_type=jnp.float32).astype(jnp.bfloat16)
    cluster_qkv = jnp.dot(normed, w_cluster, preferred_element_type=jnp.float32).astype(
        jnp.bfloat16
    )
    member_int, position, per_task = route_plan(assignment, cluster_count)
    send_counts = per_task.reshape(shards, task_slots)
    qkv_heads = cluster_qkv.reshape(tok_rows, HC, 3 * HD)
    rim_rows = shifted(local_qkv[tok_rows - WIN :, head_width:], ("sx", "sy"), 1)
    base_row = lax.axis_index(("sx", "sy")) * tok_rows
    local_mix = window_attention(local_qkv, rim_rows, base_row, tok_rows)
    offsets = (jnp.cumsum(send_counts, axis=1) - send_counts).reshape(HC, cluster_count)
    offset_of = jnp.sum(member_int * offsets[None, :, :], axis=2)
    groups_head = cluster_count // task_slots
    region = groups_head * pool_size
    local_group = assignment // task_slots
    slot_local = local_group * pool_size + offset_of + position
    table, placed = place_rows(slot_local, region, qkv_heads)
    send_pool = placed.reshape(shards, pool_size, 3 * HD)
    got_pool, got_counts = (
        lax.all_to_all(send_pool, ("sx", "sy"), split_axis=0, concat_axis=0, tiled=True),
        lax.all_to_all(send_counts, ("sx", "sy"), split_axis=0, concat_axis=0, tiled=True),
    )
    finished = pooled_tasks(got_pool, got_counts)
    came_back = lax.all_to_all(finished, ("sx", "sy"), split_axis=0, concat_axis=0, tiled=True)
    cluster_mix = collect_rows(table, came_back, region)
    combined = jnp.concatenate([local_mix, cluster_mix], axis=1)
    projected = jnp.dot(combined, w_output, preferred_element_type=jnp.float32)
    return (activations.astype(jnp.float32) + projected).astype(jnp.bfloat16)


def solution(mesh):
    in_specs = (P(("sx", "sy"), None), P(), P(), P(), P(), P(("sx", "sy"), None))
    out_specs = P(("sx", "sy"), None)
    return jax.shard_map(body, mesh=mesh, in_specs=in_specs, out_specs=out_specs, check_vma=False)
```

profile of v0, /device:TPU:0, one launch (start us, length us, event | category | flops | bytes accessed | tf_op | source)
XLA Modules:
  0.0 308.6 jit_solution(12299882472214374447)
XLA Ops:
  0.0 1.1 convert_reduce_fusion
  1.8 7.3 %all-to-all-start = ((s32[32,1,2]{2,1,0:T(1,128)}), s32[32,1,2]{2,1,0:T(1,128)S(1)}, u32[]{:S(2)}, u32[]{:S(2)}) async-start(s32[32,1,2]{2,1,0:T(1,128)} %bitcast.5), calls=%async_computation | async-start | bytes 32768 | tf_op jit(solution)/shard_map/all_to_all | solution.py:168
  9.2 1.5 fusion.23
  10.8 1.1 fusion.37
  13.7 6.6 %convolution_convert_fusion = bf16[512,3072]{1,0:T(8,128)(2,1)S(1)} fusion(bf16[1024,3072]{1,0:T(8,128)(2,1)} %param.11, bf16[512,1024]{1,0:T(8,128)(2,1)} %param.8, f32[1024]{0:T(1024)} %param.9, f32[512]{0:T(512)S(1)} %add_rsqrt_fusion), kind=kOutput, calls=%fused_computation.21 | convolution fusion | flops 3224895488 | bytes 10491904 | tf_op jit(solution)/shard_map/dot_general | solution.py:149
  20.3 4.4 %fusion.20 = bf16[8,640,384]{2,1,0:T(8,128)(2,1)} fusion(bf16[64,8,8,384]{3,2,1,0:T(8,128)(2,1)S(1)} %bitcast.70, s32[8,512]{1,0:T(8,128)S(1)} %fusion.57), kind=kOutput, calls=%fused_computation.32 | convolution fusion | flops 2017853440 | bytes 7094272 | tf_op jit(solution)/shard_map/hst,thf->hsf/dot_general | solution.py:123
  24.7 5.9 %all-to-all-start.1 = ((bf16[32,160,384]{2,1,0:T(8,128)(2,1)}), bf16[32,160,384]{2,1,0:T(8,128)(2,1)}, u32[]{:S(2)}, u32[]{:S(2)}) async-start(bf16[32,160,384]{2,1,0:T(8,128)(2,1)} %bitcast.66), calls=%async_computation.1 | async-start | bytes 7864320 | tf_op jit(solution)/shard_map/all_to_all | solution.py:167
  30.7 3.1 %convolution_convert_fusion.1 = bf16[512,1536]{1,0:T(8,128)(2,1)S(1)} fusion(bf16[1024,1536]{1,0:T(8,128)(2,1)S(1)} %copy-done, bf16[512,1024]{1,0:T(8,128)(2,1)} %param.8, f32[1024]{0:T(1024)S(1)} %copy-done.7, f32[512]{0:T(512)S(1)} %add_rsqrt_fusion), kind=kOutput, calls=%fused_computation.31 | convolution fusion | flops 1613496320 | bytes 5773312 | tf_op jit(solution)/shard_map/dot_general | solution.py:148
  33.8 1.2 copy-done.1
  35.0 1.1 slice.31
  36.2 3.1 %collective-permute-start = (bf16[512,1024]{1,0:T(8,128)(2,1)}, bf16[512,1024]{1,0:T(8,128)(2,1)}, u32[]{:S(2)}, u32[]{:S(2)}) collective-permute-start(bf16[512,1024]{1,0:T(8,128)(2,1)} %slice.31), channel_id=1, source_target_pairs={{0,1},{1,2},{2,3},{3,4},{4,5},{5,6},{6,7},{7,8},{8,9},{9,10},{10,1... | collective-permute-start | bytes 3145736 | tf_op jit(solution)/shard_map/ppermute | solution.py:19
  39.3 1.3 fusion.28
  40.9 78.4 %all-to-all-done.1 = bf16[32,160,384]{2,1,0:T(8,128)(2,1)} async-done(((bf16[32,160,384]{2,1,0:T(8,128)(2,1)}), bf16[32,160,384]{2,1,0:T(8,128)(2,1)}, u32[]{:S(2)}, u32[]{:S(2)}) %all-to-all-start.1) | async-done | bytes 3932192 | tf_op jit(solution)/shard_map/all_to_all | solution.py:167
  119.3 4.0 %fusion.63 = (bf16[5120,128]{1,0:T(8,128)(2,1)}, bf16[5120,128]{1,0:T(8,128)(2,1)}, bf16[5120,128]{1,0:T(8,128)(2,1)}) fusion(bf16[5120,384]{1,0:T(8,128)(2,1)} %bitcast.13), kind=kLoop, calls=%fused_computation.93 | loop fusion | bytes 7864320 | tf_op jit(solution)/shard_map/slice | solution.py:73
  123.3 138.2 %while.2 = (s32[]{:T(128)}, bf16[16,320,128]{2,1,0:T(8,128)(2,1)}, s32[16]{0:T(128)S(1)}, s32[5120]{0:T(1024)S(1)}, s32[5120]{0:T(1024)S(1)}, /*index=5*/bf16[51...) while((s32[]{:T(128)}, bf16[16,320,128]{2,1,0:T(8,128)(2,1)}, ...), condition=%wide.region_12.13_spmd, body=%wide.region_9.12_spmd.sunk | while | flops 853646720 | bytes 27719884 | solution.py:87
  126.1 2.7 fusion.79
  128.8 1.0 fusion.80
  130.1 1.8 fusion.81
  134.7 2.7 fusion.79
  137.4 1.0 fusion.80
  138.7 1.9 fusion.81
  143.4 2.7 fusion.79
  146.1 1.0 fusion.80
  147.4 1.8 fusion.81
  152.0 2.7 fusion.79
  156.0 1.8 fusion.81
  160.6 2.7 fusion.79
  164.7 1.8 fusion.81
  169.3 2.7 fusion.79
  173.3 1.9 fusion.81
  177.9 2.7 fusion.79
  181.9 1.8 fusion.81
  186.5 2.7 fusion.79
  190.6 1.8 fusion.81
  195.2 2.7 fusion.79
  199.2 1.9 fusion.81
  203.8 2.7 fusion.79
  207.8 1.8 fusion.81
  212.4 2.7 fusion.79
  215.1 1.0 fusion.80
  216.5 1.8 fusion.81
  221.1 2.7 fusion.79
  223.8 1.0 fusion.80
  225.1 1.8 fusion.81
  229.7 2.7 fusion.79
  232.4 1.0 fusion.80
  233.7 1.9 fusion.81
  238.3 2.7 fusion.79
  242.4 1.8 fusion.81
  247.0 2.7 fusion.79
  251.0 1.9 fusion.81
  255.6 2.7 fusion.79
  258.3 1.0 fusion.80
  259.6 1.8 fusion.81
  261.5 3.6 %broadcast_select_fusion = bf16[32,160,128]{2,1,0:T(8,128)(2,1)} fusion(bf16[32,160,128]{2,1,0:T(8,128)(2,1)} %bitcast.67, pred[32,160]{1,0:T(8,128)(4,1)S(1)} %broadcast_compare_fusion), kind=kLoop, calls=%fused_computation.48 | loop fusion | flops 655360 | bytes 2626560 | tf_op jit(solution)/shard_map/jit(_where)/select_n | solution.py:101
  265.1 5.4 %all-to-all-start.2 = ((bf16[32,160,128]{2,1,0:T(8,128)(2,1)}), bf16[32,160,128]{2,1,0:T(8,128)(2,1)}, u32[]{:S(2)}, u32[]{:S(2)}) async-start(bf16[32,160,128]{2,1,0:T(8,128)(2,1)} %broadcast_select_fusion), calls=%async_computation.2 | async-start | bytes 2621440 | tf_op jit(solution)/shard_map/all_to_all | solution.py:171
  270.5 3.1 %fusion.42 = (bf16[128,4,8,128]{3,2,1,0:T(8,128)(2,1)}, bf16[1024,512]{1,0:T(8,128)(2,1)}) fusion(bf16[512,1024]{1,0:T(8,128)(2,1)} %slice.31, bf16[512,1024]{1,0:T(8,128)(2,1)} %collective-permute-done), kind=kLoop, calls=%fused_computation.57 | loop fusion | flops 4194304 | bytes 4194304
  273.6 2.3 copy.36
  275.8 2.7 fusion.39
  278.6 6.0 %fusion.64 = (f32[4,512]{1,0:T(4,128)S(1)}, f32[4,512,1024]{2,1,0:T(8,128)}) fusion(f32[4,512,1024]{2,1,0:T(8,128)S(1)} %fusion.39, pred[512,1024]{1,0:T(8,128)(4,1)S(1)} %copy-done.5), kind=kOutput, calls=%fused_computation.94 | output fusion | flops 12583935 | bytes 17309696 | tf_op jit(solution)/shard_map/while/body/eval_jaxpr/sub | solution.py:30
  284.5 5.8 %fusion.36 = bf16[4,128,512]{2,1,0:T(8,128)(2,1)} fusion(bf16[1024,4,128]{0,2,1:T(8,128)(2,1)S(1)} %bitcast.68, f32[4,512,1024]{2,1,0:T(8,128)} %get-tuple-element.87, f32[4,512]{1,0:T(4,128)S(1)} %get-tuple-element.86), kind=kOutput, calls=%fused_computation.49 | convolution fusion | flops 541327360 | bytes 9969664 | tf_op jit(solution)/shard_map/while/body/eval_jaxpr/hqk,khd->qhd/dot_general | solution.py:58
  290.3 11.8 %all-to-all-done.2 = bf16[32,160,128]{2,1,0:T(8,128)(2,1)} async-done(((bf16[32,160,128]{2,1,0:T(8,128)(2,1)}), bf16[32,160,128]{2,1,0:T(8,128)(2,1)}, u32[]{:S(2)}, u32[]{:S(2)}) %all-to-all-start.2) | async-done | bytes 1310752 | tf_op jit(solution)/shard_map/all_to_all | solution.py:171
  302.1 3.6 %fusion.33 = bf16[8,128,512]{2,1,0:T(8,128)(2,1)S(1)} fusion(bf16[8,640,128]{2,1,0:T(8,128)(2,1)} %bitcast.15, s32[8,512]{1,0:T(8,128)S(1)} %fusion.57), kind=kOutput, calls=%fused_computation.47 | convolution fusion | flops 674234368 | bytes 2375680 | tf_op jit(solution)/shard_map/hst,hsf->thf/dot_general | solution.py:131
  305.8 2.8 fusion.26
  (110 shorter events, 28.5 us)
Async XLA Ops:
  0.0 30.7 %copy-start = (bf16[1024,1536]{1,0:T(8,128)(2,1)S(1)}, bf16[1024,1536]{1,0:T(8,128)(2,1)}, u32[]{:S(2)}) copy-start(bf16[1024,1536]{1,0:T(8,128)(2,1)} %param.10) | copy-start | bytes 9437188
  1.8 22.9 %all-to-all-start = ((s32[32,1,2]{2,1,0:T(1,128)}), s32[32,1,2]{2,1,0:T(1,128)S(1)}, u32[]{:S(2)}, u32[]{:S(2)}) async-start(s32[32,1,2]{2,1,0:T(1,128)} %bitcast.5), calls=%async_computation | async-start | bytes 32768 | tf_op jit(solution)/shard_map/all_to_all | solution.py:168
  24.7 6.0 %copy-start.7 = (f32[1024]{0:T(1024)S(1)}, f32[1024]{0:T(1024)}, u32[]{:S(2)}) copy-start(f32[1024]{0:T(1024)} %param.9) | copy-start | bytes 12292
  24.7 94.6 %all-to-all-start.1 = ((bf16[32,160,384]{2,1,0:T(8,128)(2,1)}), bf16[32,160,384]{2,1,0:T(8,128)(2,1)}, u32[]{:S(2)}, u32[]{:S(2)}) async-start(bf16[32,160,384]{2,1,0:T(8,128)(2,1)} %bitcast.66), calls=%async_computation.1 | async-start | bytes 7864320 | tf_op jit(solution)/shard_map/all_to_all | solution.py:167
  33.8 1.2 copy-start.1
  36.2 234.3 %collective-permute-start = (bf16[512,1024]{1,0:T(8,128)(2,1)}, bf16[512,1024]{1,0:T(8,128)(2,1)}, u32[]{:S(2)}, u32[]{:S(2)}) collective-permute-start(bf16[512,1024]{1,0:T(8,128)(2,1)} %slice.31), channel_id=1, source_target_pairs={{0,1},{1,2},{2,3},{3,4},{4,5},{5,6},{6,7},{7,8},{8,9},{9,10},{10,1... | collective-permute-start | bytes 3145736 | tf_op jit(solution)/shard_map/ppermute | solution.py:19
  128.8 1.3 copy-start.2
  137.4 1.3 copy-start.2
  146.1 1.3 copy-start.2
  154.7 1.3 copy-start.2
  163.3 1.3 copy-start.2
  172.0 1.3 copy-start.2
  180.6 1.3 copy-start.2
  189.2 1.3 copy-start.2
  197.9 1.3 copy-start.2
  206.5 1.3 copy-start.2
  215.1 1.3 copy-start.2
  223.8 1.3 copy-start.2
  232.4 1.3 copy-start.2
  241.0 1.3 copy-start.2
  249.7 1.3 copy-start.2
  258.3 1.3 copy-start.2
  265.1 37.1 %all-to-all-start.2 = ((bf16[32,160,128]{2,1,0:T(8,128)(2,1)}), bf16[32,160,128]{2,1,0:T(8,128)(2,1)}, u32[]{:S(2)}, u32[]{:S(2)}) async-start(bf16[32,160,128]{2,1,0:T(8,128)(2,1)} %broadcast_select_fusion), calls=%async_computation.2 | async-start | bytes 2621440 | tf_op jit(solution)/shard_map/all_to_all | solution.py:171
  275.8 2.7 copy-start.5
  278.6 6.0 %copy-start.4 = (bf16[1024,512]{0,1:T(8,128)(2,1)S(1)}, bf16[1024,512]{0,1:T(8,128)(2,1)}, u32[]{:S(2)}) copy-start(bf16[1024,512]{0,1:T(8,128)(2,1)} %copy.36) | copy-start | bytes 3145732
  302.1 3.7 %copy-start.3 = (bf16[512,1024]{1,0:T(8,128)(2,1)S(1)}, bf16[512,1024]{1,0:T(8,128)(2,1)}, u32[]{:S(2)}) copy-start(bf16[512,1024]{1,0:T(8,128)(2,1)} %param.8) | copy-start | bytes 3145732
  302.1 3.7 %copy-start.6 = (bf16[1536,1024]{1,0:T(8,128)(2,1)S(1)}, bf16[1536,1024]{1,0:T(8,128)(2,1)}, u32[]{:S(2)}) copy-start(bf16[1536,1024]{1,0:T(8,128)(2,1)} %param.12) | copy-start | bytes 9437188
  302.1 3.7 %copy-start.8 = (bf16[4,128,512]{2,1,0:T(8,128)(2,1)S(1)}, bf16[4,128,512]{2,1,0:T(8,128)(2,1)}, u32[]{:S(2)}) copy-start(bf16[4,128,512]{2,1,0:T(8,128)(2,1)} %fusion.36) | copy-start | bytes 1572868
where the time goes:
time: 311 us; the launch traced here: 309 us
  matrix products  103 us (33%)
  waiting for transfers between devices  90.2 us (29%)
  other arithmetic  35.1 us (11%)
  loops' own time  32.7 us (11%)
  local copies, waits for them, and re-layouts  25.9 us (8%)
  starting transfers between devices  21.8 us (7%)
    all_to_all x1, waiting for transfers between devices, body(): lax.all_to_all(send_pool, ('sx', 'sy'), split_axis=0, concat_axis=0, tile...  78.4 us
    dot_general x16, matrix products, tagged_one_block(): jnp.einsum('qd,kd->qk', query_block, key_rows, preferred_element_type=jnp...  43.2 us
    another operation x1, loops' own time, tagged_attention(): return lax.map(tagged_one_block, starts).reshape(total, HD)  32.7 us
    dot_general x16, matrix products, tagged_one_block(): jnp.dot(weights, value_rows, preferred_element_type=jnp.float32)  29.5 us
    reduce_sum x16, other arithmetic, normalize_rows(): jnp.sum(raised, axis=-1, keepdims=True)  16.7 us
    all_to_all x1, waiting for transfers between devices, body(): lax.all_to_all(finished, ('sx', 'sy'), split_axis=0, concat_axis=0, tiled...  11.8 us
    dynamic_slice x16, local copies, waits for them, and re-layouts, tagged_attention(): return lax.map(tagged_one_block, starts).reshape(total, HD)  10.5 us
    all_to_all x1, starting transfers between devices, body(): lax.all_to_all(send_counts, ('sx', 'sy'), split_axis=0, concat_axis=0, ti...  7.33 us
  transfers between devices with their start and end apart: 4, of which 2 were waited for; matrix products, arithmetic and copies ran while one was open for 49% of the time, Pallas kernels for 0%

commit v1 on v0

--- a/solution.py
+++ b/solution.py
@@ -1,6 +1,10 @@
+import functools
+
 import jax
 import jax.numpy as jnp
 from jax import lax
+from jax.experimental import pallas as pl
+from jax.experimental.pallas import tpu as pltpu
 from jax.sharding import PartitionSpec as P
 
 HL = 4
@@ -62,43 +66,111 @@
     return lax.map(window_one_block, starts).reshape(tok_rows, head_width)
 
 
-def tagged_attention(rows, query_tags, key_tags):
-    score_scale = HD ** (-0.5)
-    total = rows.shape[0]
-    block_rows = total
-    while block_rows > 512 and block_rows % 2 == 0:
-        block_rows = block_rows // 2
-    queries = rows[:, :HD]
-    key_rows = rows[:, HD : 2 * HD]
-    value_rows = rows[:, 2 * HD :]
-
-    def tagged_one_block(first_row):
-        query_block = lax.dynamic_slice_in_dim(queries, first_row, block_rows, 0)
-        tag_block = lax.dynamic_slice_in_dim(query_tags, first_row, block_rows, 0)
-        scores = (
-            jnp.einsum("qd,kd->qk", query_block, key_rows, preferred_element_type=jnp.float32)
-            * score_scale
-        )
-        scores = jnp.where(tag_block[:, None] == key_tags[None, :], scores, -1e30)
-        weights = normalize_rows(scores)
-        return jnp.dot(weights, value_rows, preferred_element_type=jnp.float32).astype(jnp.bfloat16)
-
-    starts = jnp.arange(total // block_rows, dtype=jnp.int32) * block_rows
-    return lax.map(tagged_one_block, starts).reshape(total, HD)
-
-
-def pooled_tasks(pool_rows, pool_counts):
+def task_kernel(sources, pool_size, task_slots, run, counts_ref, pool_ref, out_ref, *scratch):
+    flat, packed, exact, mixed, spread = scratch[:3], scratch[3:6], scratch[6:9], scratch[9], scratch[10]
+    total = sources * pool_size
+    rows = task_slots * CSIZE
+    chunk = total // 8
+    exponent_scale = HD ** (-0.5) * 1.4426950408889634
+
+    @pl.loop(0, 8)
+    def _(step):
+        start = pl.multiple_of(step * chunk, chunk)
+        for part in range(3):
+            flat[part][pl.ds(start, chunk), :] = pool_ref[
+                pl.ds(start, chunk), part * HD : (part + 1) * HD
+            ].astype(jnp.float32)
+
+    def before(source, task):
+        first = source * pool_size
+        for earlier in range(task):
+            first = first + counts_ref[source * task_slots + earlier]
+        return first
+
+    for task in range(task_slots):
+
+        def pack(source, place, task=task):
+            first = before(source, task)
+            for part in range(3):
+                packed[part][pl.ds(place, run), :] = flat[part][pl.ds(first, run), :]
+            return place + counts_ref[source * task_slots + task]
+
+        lax.fori_loop(0, sources, pack, jnp.int32(task * CSIZE))
+
+    @pl.loop(0, 8)
+    def _(step):
+        start = pl.multiple_of(step * (rows // 8), rows // 8)
+        for part in range(3):
+            exact[part][pl.ds(start, rows // 8), :] = packed[part][
+                pl.ds(start, rows // 8), :
+            ].astype(jnp.bfloat16)
+
+    block_rows = 256
+    together = 2
+
+    @pl.loop(0, rows // (block_rows * together))
+    def _(step):
+        base = step * (block_rows * together)
+        key_start = pl.multiple_of(base // CSIZE * CSIZE, CSIZE)
+        keys = exact[1][pl.ds(key_start, CSIZE), :]
+        values = exact[2][pl.ds(key_start, CSIZE), :]
+        for part in range(together):
+            start = pl.multiple_of(base + part * block_rows, block_rows)
+            scores = lax.dot_general(
+                exact[0][pl.ds(start, block_rows), :],
+                keys,
+                (((1,), (1,)), ((), ())),
+                preferred_element_type=jnp.float32,
+            )
+            highest = jnp.max(scores, axis=-1, keepdims=True)
+            raised = jnp.exp2((scores - highest) * exponent_scale)
+            inverse = 1.0 / jnp.sum(raised, axis=-1, keepdims=True)
+            weights = (raised * inverse).astype(jnp.bfloat16)
+            mixed[pl.ds(start, block_rows), :] = jnp.dot(
+                weights, values, preferred_element_type=jnp.float32
+            )
+
+    mixed[pl.ds(rows, run), :] = jnp.zeros((run, HD), jnp.float32)
+    spread[...] = jnp.zeros_like(spread)
+
+    def unpack(source, places):
+        after = []
+        for task in range(task_slots):
+            first = before(source, task)
+            spread[pl.ds(first, run), :] = mixed[pl.ds(places[task], run), :]
+            after.append(places[task] + counts_ref[source * task_slots + task])
+        return tuple(after)
+
+    lax.fori_loop(
+        0, sources, unpack, tuple(jnp.int32(task * CSIZE) for task in range(task_slots))
+    )
+    out_ref[...] = spread[pl.ds(0, total), :].astype(jnp.bfloat16)
+
+
+def pooled_tasks(pool_rows, pool_counts, run):
     sources, pool_size = (pool_rows.shape[0], pool_rows.shape[1])
     task_slots = pool_counts.shape[1]
-    bounds = jnp.cumsum(pool_counts, axis=1)
-    slot_ids = jnp.arange(pool_size, dtype=jnp.int32)
-    task_of = jnp.sum(
-        (bounds[:, None, :] <= slot_ids[None, :, None]).astype(jnp.int32), axis=2
-    ).reshape(-1)
-    alive = task_of < task_slots
-    key_tags = jnp.where(alive, task_of, -1)
-    result = tagged_attention(pool_rows.reshape(-1, 3 * HD), task_of, key_tags)
-    result = jnp.where(alive[:, None], result, jnp.zeros_like(result))
+    total = sources * pool_size
+    rows = task_slots * CSIZE
+    wide = [pltpu.VMEM((total + run, HD), jnp.float32)] * 3
+    tight = [pltpu.VMEM((rows + run, HD), jnp.float32)] * 3
+    exact = [pltpu.VMEM((rows, HD), jnp.bfloat16)] * 3
+    result = pl.pallas_call(
+        functools.partial(task_kernel, sources, pool_size, task_slots, run),
+        out_shape=jax.ShapeDtypeStruct((total, HD), jnp.bfloat16),
+        in_specs=[
+            pl.BlockSpec(memory_space=pltpu.SMEM),
+            pl.BlockSpec(memory_space=pltpu.VMEM),
+        ],
+        out_specs=pl.BlockSpec(memory_space=pltpu.VMEM),
+        scratch_shapes=wide + tight + exact + [tight[0], wide[0]],
+        compiler_params=pltpu.CompilerParams(vmem_limit_bytes=56 * 1024 * 1024),
+        cost_estimate=pl.CostEstimate(
+            flops=4 * task_slots * CSIZE * CSIZE * HD,
+            bytes_accessed=total * 4 * HD * 2,
+            transcendentals=task_slots * CSIZE * CSIZE,
+        ),
+    )(pool_counts.reshape(-1), pool_rows.reshape(total, 3 * HD))
     return result.reshape(sources, pool_size, HD)
 
 
@@ -163,11 +235,12 @@
     slot_local = local_group * pool_size + offset_of + position
     table, placed = place_rows(slot_local, region, qkv_heads)
     send_pool = placed.reshape(shards, pool_size, 3 * HD)
-    got_pool, got_counts = (
-        lax.all_to_all(send_pool, ("sx", "sy"), split_axis=0, concat_axis=0, tiled=True),
-        lax.all_to_all(send_counts, ("sx", "sy"), split_axis=0, concat_axis=0, tiled=True),
-    )
-    finished = pooled_tasks(got_pool, got_counts)
+    got_pool = lax.all_to_all(send_pool, ("sx", "sy"), split_axis=0, concat_axis=0, tiled=True)
+    every_count = lax.all_gather(per_task, ("sx", "sy"), axis=0)
+    own_task = lax.axis_index(("sx", "sy")) * task_slots
+    got_counts = lax.dynamic_slice_in_dim(every_count, own_task, task_slots, 1)
+    run = (mean_rows + mean_rows // 2 + mean_rows // 4 + 7) // 8 * 8
+    finished = pooled_tasks(got_pool, got_counts, run)
     came_back = lax.all_to_all(finished, ("sx", "sy"), split_axis=0, concat_axis=0, tiled=True)
     cluster_mix = collect_rows(table, came_back, region)
     combined = jnp.concatenate([local_mix, cluster_mix], axis=1)

time: 311 us -> 215 us (0.69)
  blocking collectives: 0 us -> 97.3 us
  waiting for transfers between devices: 90.2 us -> 12 us
  matrix products: 103 us -> 30.1 us
  loops' own time: 32.7 us -> 0 us
  Pallas kernels: 0 us -> 23.5 us
  other arithmetic: 35.1 us -> 14.7 us
  local copies, waits for them, and re-layouts: 25.9 us -> 5.71 us
  starting transfers between devices: 21.8 us -> 31.2 us
    all_gather x0 -> x1, blocking collectives: none -> 97.3 us  [body(): every_count = lax.all_gather(per_task, ('sx', 'sy'), axis=0)]
    all_to_all x1, waiting for transfers between devices: 78.4 us -> 0.01 us  [body(): lax.all_to_all(send_pool, ('sx', 'sy'), split_axis=0, concat_axis=0, tile...]
    dot_general x32 -> x0, matrix products: 72.7 us -> none  [the longest x16 43.2 us: tagged_one_block(): jnp.einsum('qd,kd->qk', query_block, key_rows, preferred_element_type=jnp...]
    another operation x1 -> x0, loops' own time: 32.7 us -> none  [tagged_attention(): return lax.map(tagged_one_block, starts).reshape(total, HD)]
    pallas_call x0 -> x1, Pallas kernels: none -> 23.5 us  [pooled_tasks(): pl.pallas_call(functools.partial(task_kernel, sources, pool_size, task_sl...]
    reduce_sum x17 -> x0, other arithmetic: 16.7 us -> none  [the longest x16 16.7 us: normalize_rows(): jnp.sum(raised, axis=-1, keepdims=True)]
    all_to_all x1, starting transfers between devices: 5.39 us -> 20.7 us  [body(): lax.all_to_all(finished, ('sx', 'sy'), split_axis=0, concat_axis=0, tiled...]
    dynamic_slice x32 -> x1, local copies, waits for them, and re-layouts: 11.7 us -> 0.12 us  [body(): got_counts = lax.dynamic_slice_in_dim(every_count, own_task, task_slots, 1)]
  transfers between devices with their start and end apart: 4 -> 3, of which waited for: 2 -> 1; matrix products, arithmetic and copies ran while one was open for 49% -> 12% of each run, Pallas kernels for 0% -> 11%
where the time goes in v1:
time: 215 us
  blocking collectives  97.3 us (45%)
  starting transfers between devices  31.2 us (15%)
  matrix products  30.1 us (14%)
  Pallas kernels  23.5 us (11%)
  other arithmetic  14.7 us (7%)
  waiting for transfers between devices  12 us (6%)
  local copies, waits for them, and re-layouts  5.71 us (3%)
    all_gather x1, blocking collectives, body(): every_count = lax.all_gather(per_task, ('sx', 'sy'), axis=0)  97.3 us
    pallas_call x1, Pallas kernels, pooled_tasks(): pl.pallas_call(functools.partial(task_kernel, sources, pool_size, task_sl...  23.5 us
    all_to_all x1, starting transfers between devices, body(): lax.all_to_all(finished, ('sx', 'sy'), split_axis=0, concat_axis=0, tiled...  20.7 us
    all_to_all x1, waiting for transfers between devices, body(): lax.all_to_all(finished, ('sx', 'sy'), split_axis=0, concat_axis=0, tiled...  12 us
    all_to_all x1, starting transfers between devices, body(): lax.all_to_all(send_pool, ('sx', 'sy'), split_axis=0, concat_axis=0, tile...  7.44 us
    dot_general x1, matrix products, body(): jnp.dot(normed, w_cluster, preferred_element_type=jnp.float32)  6.64 us
    sub x1, other arithmetic, normalize_rows(): raised = jnp.exp(scores - highest)  5.97 us
    dot_general x1, matrix products, window_one_block(): jnp.einsum('hqk,khd->qhd', weights, value_block, preferred_element_type=j...  5.81 us
  transfers between devices with their start and end apart: 3, of which 1 were waited for; matrix products, arithmetic and copies ran while one was open for 12% of the time, Pallas kernels for 11%

profile of v1, /device:TPU:0, one launch (start us, length us, event | category | flops | bytes accessed | tf_op | source)
XLA Modules:
  0.0 214.7 jit_solution(1133560371981824973)
XLA Ops:
  0.0 0.0 copy-start
  0.0 1.7 fusion.15
  1.7 0.9 convert_reduce_fusion
  2.6 0.1 reshape_reshape.3
  2.7 0.2 reduce_window_sum.13
  2.8 0.1 reduce_window_sum.14
  2.9 0.8 select_reduce_fusion
  3.8 0.1 eq.43
  3.8 1.1 fusion.29
  4.9 0.7 fusion.49
  5.7 6.6 %convolution_convert_fusion = bf16[512,3072]{1,0:T(8,128)(2,1)S(1)} fusion(bf16[1024,3072]{1,0:T(8,128)(2,1)} %param.9, bf16[512,1024]{1,0:T(8,128)(2,1)} %param.6, f32[1024]{0:T(1024)} %param.7, f32[512]{0:T(512)S(1)} %add_rsqrt_fusion), kind=kOutput, calls=%fused_computation.10 | convolution fusion | flops 3224895488 | bytes 10491904 | tf_op jit(solution)/shard_map/dot_general | solution.py:221
  12.3 4.4 %fusion.12 = bf16[8,640,384]{2,1,0:T(8,128)(2,1)} fusion(bf16[64,8,8,384]{3,2,1,0:T(8,128)(2,1)S(1)} %bitcast.52, s32[8,512]{1,0:T(8,128)S(1)} %fusion.49), kind=kOutput, calls=%fused_computation.21 | convolution fusion | flops 2017853440 | bytes 7094272 | tf_op jit(solution)/shard_map/hst,thf->hsf/dot_general | solution.py:195
  16.7 0.0 copy-start.6
  16.7 7.4 %all-to-all-start = ((bf16[32,160,384]{2,1,0:T(8,128)(2,1)}), bf16[32,160,384]{2,1,0:T(8,128)(2,1)}, u32[]{:S(2)}, u32[]{:S(2)}) async-start(bf16[32,160,384]{2,1,0:T(8,128)(2,1)} %bitcast.49), calls=%async_computation | async-start | bytes 7864320 | tf_op jit(solution)/shard_map/all_to_all | solution.py:238
  24.1 0.0 copy-done
  24.2 0.0 copy-done.6
  24.2 3.1 %convolution_convert_fusion.1 = bf16[512,1536]{1,0:T(8,128)(2,1)S(1)} fusion(bf16[1024,1536]{1,0:T(8,128)(2,1)S(1)} %copy-done, bf16[512,1024]{1,0:T(8,128)(2,1)} %param.6, f32[1024]{0:T(1024)S(1)} %copy-done.6, f32[512]{0:T(512)S(1)} %add_rsqrt_fusion), kind=kOutput, calls=%fused_computation.20 | convolution fusion | flops 1613496320 | bytes 5773312 | tf_op jit(solution)/shard_map/dot_general | solution.py:220
  27.3 0.0 copy-start.1
  27.3 1.2 copy-done.1
  28.5 1.1 slice.19
  29.7 3.1 %collective-permute-start = (bf16[512,1024]{1,0:T(8,128)(2,1)}, bf16[512,1024]{1,0:T(8,128)(2,1)}, u32[]{:S(2)}, u32[]{:S(2)}) collective-permute-start(bf16[512,1024]{1,0:T(8,128)(2,1)} %slice.19), channel_id=1, source_target_pairs={{0,1},{1,2},{2,3},{3,4},{4,5},{5,6},{6,7},{7,8},{8,9},{9,10},{10,1... | collective-permute-start | bytes 3145736 | tf_op jit(solution)/shard_map/ppermute | solution.py:23
  32.7 0.1 reshape.137
  32.8 97.3 %all-gather = s32[32,1,64]{2,1,0:T(1,128)S(1)} all-gather(s32[1,1,64]{2,1,0:T(1,128)S(1)} %reshape.137), channel_id=1, replica_groups=mesh['sx'=8,'sy'=4] {'sx','sy'}, dimensions={0}, use_global_device_ids=true | all-gather | bytes 8448 | tf_op jit(solution)/shard_map/all_gather | solution.py:239
  130.1 0.1 dynamic-slice_reduce_fusion
  130.3 0.7 reshape.130.counts_ref
  130.9 1.3 fusion.20
  132.2 0.0 all-to-all-done
  132.2 23.5 %shard_map.64 = bf16[5120,128]{1,0:T(8,128)(2,1)} custom-call(s32[64]{0:T(128)} %reshape.130.counts_ref, bf16[5120,384]{1,0:T(8,128)(2,1)} %bitcast.9.pool_ref), custom_call_target="tpu_custom_call" | custom-call | flops 4294967296 | bytes 5242880 | tf_op jit(solution)/shard_map/pallas_call | solution.py:158
  155.7 20.7 %all-to-all-start.1 = ((bf16[32,160,128]{2,1,0:T(8,128)(2,1)}), bf16[32,160,128]{2,1,0:T(8,128)(2,1)}, u32[]{:S(2)}, u32[]{:S(2)}) async-start(bf16[32,160,128]{2,1,0:T(8,128)(2,1)} %bitcast.50), calls=%async_computation.1 | async-start | bytes 2621440 | tf_op jit(solution)/shard_map/all_to_all | solution.py:244
  176.4 0.0 collective-permute-done
  176.4 3.1 %fusion.34 = (bf16[128,4,8,128]{3,2,1,0:T(8,128)(2,1)}, bf16[1024,512]{1,0:T(8,128)(2,1)}) fusion(bf16[512,1024]{1,0:T(8,128)(2,1)} %slice.19, bf16[512,1024]{1,0:T(8,128)(2,1)} %collective-permute-done), kind=kLoop, calls=%fused_computation.45 | loop fusion | flops 4194304 | bytes 4194304
  179.5 2.3 %copy.22 = bf16[1024,512]{0,1:T(8,128)(2,1)} copy(bf16[1024,512]{1,0:T(8,128)(2,1)} %get-tuple-element.14) | data formatting | bytes 2097152 | tf_op jit(solution)/shard_map/while/body/eval_jaxpr/reshape | solution.py:48
  181.8 0.0 copy-start.4
  181.8 2.7 %fusion.31 = f32[4,512,1024]{2,1,0:T(8,128)S(1)} fusion(bf16[128,4,8,128]{3,2,1,0:T(8,128)(2,1)} %get-tuple-element.13, bf16[512,1536]{1,0:T(8,128)(2,1)} %copy-done.1), kind=kOutput, calls=%fused_computation.41 | convolution fusion | flops 536870912 | bytes 9961472 | tf_op jit(solution)/shard_map/while/body/eval_jaxpr/qhd,khd->hqk/dot_general | solution.py:50
  184.5 0.0 copy-done.4
  184.5 0.0 copy-start.3
  184.5 6.0 %fusion.54 = (f32[4,512]{1,0:T(4,128)S(1)}, f32[4,512,1024]{2,1,0:T(8,128)}) fusion(f32[4,512,1024]{2,1,0:T(8,128)S(1)} %fusion.31, pred[512,1024]{1,0:T(8,128)(4,1)S(1)} %copy-done.4), kind=kOutput, calls=%fused_computation.76 | output fusion | flops 12583935 | bytes 17309696 | tf_op jit(solution)/shard_map/while/body/eval_jaxpr/sub | solution.py:34
  190.4 0.0 copy-done.3
  190.5 5.8 %fusion.28 = bf16[4,128,512]{2,1,0:T(8,128)(2,1)} fusion(bf16[1024,4,128]{0,2,1:T(8,128)(2,1)S(1)} %bitcast.51, f32[4,512,1024]{2,1,0:T(8,128)} %get-tuple-element.22, f32[4,512]{1,0:T(4,128)S(1)} %get-tuple-element.20), kind=kOutput, calls=%fused_computation.37 | convolution fusion | flops 541327360 | bytes 9969664 | tf_op jit(solution)/shard_map/while/body/eval_jaxpr/hqk,khd->qhd/dot_general | solution.py:62
  196.3 12.0 %all-to-all-done.1 = bf16[32,160,128]{2,1,0:T(8,128)(2,1)} async-done(((bf16[32,160,128]{2,1,0:T(8,128)(2,1)}), bf16[32,160,128]{2,1,0:T(8,128)(2,1)}, u32[]{:S(2)}, u32[]{:S(2)}) %all-to-all-start.1) | async-done | bytes 1310752 | tf_op jit(solution)/shard_map/all_to_all | solution.py:244
  208.3 0.0 copy-start.2
  208.3 0.0 copy-start.5
  208.3 0.0 copy-start.7
  208.3 3.6 %fusion.25 = bf16[8,128,512]{2,1,0:T(8,128)(2,1)S(1)} fusion(bf16[8,640,128]{2,1,0:T(8,128)(2,1)} %bitcast.11, s32[8,512]{1,0:T(8,128)S(1)} %fusion.49), kind=kOutput, calls=%fused_computation.36 | convolution fusion | flops 674234368 | bytes 2375680 | tf_op jit(solution)/shard_map/hst,hsf->thf/dot_general | solution.py:203
  211.9 0.0 copy-done.2
  211.9 0.0 copy-done.5
  211.9 0.0 copy-done.7
  212.0 2.8 %fusion.18 = bf16[512,1024]{1,0:T(8,128)(2,1)} fusion(bf16[512,1024]{1,0:T(8,128)(2,1)S(1)} %copy-done.2, bf16[1536,1024]{1,0:T(8,128)(2,1)S(1)} %copy-done.5, bf16[512,1024]{0,1:T(8,128)(2,1)S(1)} %bitcast.53, bf16[512,512]{0,1:T(8,128)(2,1)S(1)} %bitcast.54), kind=kOutput, calls=%fused_computation.25 | convolution fusion | flops 1615331328 | bytes 6815744 | tf_op jit(solution)/shard_map/dot_general | solution.py:247
  (5 shorter events, 0.0 us)
Async XLA Ops:
  0.0 24.1 %copy-start = (bf16[1024,1536]{1,0:T(8,128)(2,1)S(1)}, bf16[1024,1536]{1,0:T(8,128)(2,1)}, u32[]{:S(2)}) copy-start(bf16[1024,1536]{1,0:T(8,128)(2,1)} %param.8) | copy-start | bytes 9437188
  16.7 7.5 %copy-start.6 = (f32[1024]{0:T(1024)S(1)}, f32[1024]{0:T(1024)}, u32[]{:S(2)}) copy-start(f32[1024]{0:T(1024)} %param.7) | copy-start | bytes 12292
  16.7 115.5 %all-to-all-start = ((bf16[32,160,384]{2,1,0:T(8,128)(2,1)}), bf16[32,160,384]{2,1,0:T(8,128)(2,1)}, u32[]{:S(2)}, u32[]{:S(2)}) async-start(bf16[32,160,384]{2,1,0:T(8,128)(2,1)} %bitcast.49), calls=%async_computation | async-start | bytes 7864320 | tf_op jit(solution)/shard_map/all_to_all | solution.py:238
  27.3 1.2 copy-start.1
  29.7 146.7 %collective-permute-start = (bf16[512,1024]{1,0:T(8,128)(2,1)}, bf16[512,1024]{1,0:T(8,128)(2,1)}, u32[]{:S(2)}, u32[]{:S(2)}) collective-permute-start(bf16[512,1024]{1,0:T(8,128)(2,1)} %slice.19), channel_id=1, source_target_pairs={{0,1},{1,2},{2,3},{3,4},{4,5},{5,6},{6,7},{7,8},{8,9},{9,10},{10,1... | collective-permute-start | bytes 3145736 | tf_op jit(solution)/shard_map/ppermute | solution.py:23
  155.7 52.6 %all-to-all-start.1 = ((bf16[32,160,128]{2,1,0:T(8,128)(2,1)}), bf16[32,160,128]{2,1,0:T(8,128)(2,1)}, u32[]{:S(2)}, u32[]{:S(2)}) async-start(bf16[32,160,128]{2,1,0:T(8,128)(2,1)} %bitcast.50), calls=%async_computation.1 | async-start | bytes 2621440 | tf_op jit(solution)/shard_map/all_to_all | solution.py:244
  181.8 2.7 %copy-start.4 = (pred[512,1024]{1,0:T(8,128)(4,1)S(1)}, pred[512,1024]{1,0:T(8,128)(4,1)}, u32[]{:S(2)}) copy-start(pred[512,1024]{1,0:T(8,128)(4,1)} %fusion.20) | copy-start | bytes 1572868
  184.5 6.0 %copy-start.3 = (bf16[1024,512]{0,1:T(8,128)(2,1)S(1)}, bf16[1024,512]{0,1:T(8,128)(2,1)}, u32[]{:S(2)}) copy-start(bf16[1024,512]{0,1:T(8,128)(2,1)} %copy.22) | copy-start | bytes 3145732
  208.3 3.7 %copy-start.2 = (bf16[512,1024]{1,0:T(8,128)(2,1)S(1)}, bf16[512,1024]{1,0:T(8,128)(2,1)}, u32[]{:S(2)}) copy-start(bf16[512,1024]{1,0:T(8,128)(2,1)} %param.6) | copy-start | bytes 3145732
  208.3 3.7 %copy-start.5 = (bf16[1536,1024]{1,0:T(8,128)(2,1)S(1)}, bf16[1536,1024]{1,0:T(8,128)(2,1)}, u32[]{:S(2)}) copy-start(bf16[1536,1024]{1,0:T(8,128)(2,1)} %param.10) | copy-start | bytes 9437188
  208.3 3.7 %copy-start.7 = (bf16[4,128,512]{2,1,0:T(8,128)(2,1)S(1)}, bf16[4,128,512]{2,1,0:T(8,128)(2,1)}, u32[]{:S(2)}) copy-start(bf16[4,128,512]{2,1,0:T(8,128)(2,1)} %fusion.28) | copy-start | bytes 1572868

commit v2 on v0

--- a/solution.py
+++ b/solution.py
@@ -1,7 +1,12 @@
+import functools
+
 import jax
 import jax.numpy as jnp
 from jax import lax
+from jax.experimental import pallas as pl
+from jax.experimental.pallas import tpu as pltpu
 from jax.sharding import PartitionSpec as P
+
 
 HL = 4
 HC = 8
@@ -62,44 +67,170 @@
     return lax.map(window_one_block, starts).reshape(tok_rows, head_width)
 
 
-def tagged_attention(rows, query_tags, key_tags):
-    score_scale = HD ** (-0.5)
-    total = rows.shape[0]
-    block_rows = total
-    while block_rows > 512 and block_rows % 2 == 0:
-        block_rows = block_rows // 2
-    queries = rows[:, :HD]
-    key_rows = rows[:, HD : 2 * HD]
-    value_rows = rows[:, 2 * HD :]
-
-    def tagged_one_block(first_row):
-        query_block = lax.dynamic_slice_in_dim(queries, first_row, block_rows, 0)
-        tag_block = lax.dynamic_slice_in_dim(query_tags, first_row, block_rows, 0)
-        scores = (
-            jnp.einsum("qd,kd->qk", query_block, key_rows, preferred_element_type=jnp.float32)
-            * score_scale
+BLOCK = 256
+
+
+def attend(queries, keys, values, mixed, first_row, last_row, key_start):
+    exponent_scale = HD ** (-0.5) * 1.4426950408889634
+
+    @pl.loop(first_row // BLOCK, last_row // BLOCK)
+    def _(step):
+        start = pl.multiple_of(step * BLOCK, BLOCK)
+        scores = lax.dot_general(
+            queries[pl.ds(start, BLOCK), :].astype(jnp.bfloat16),
+            keys[pl.ds(key_start, CSIZE), :],
+            (((1,), (1,)), ((), ())),
+            preferred_element_type=jnp.float32,
         )
-        scores = jnp.where(tag_block[:, None] == key_tags[None, :], scores, -1e30)
-        weights = normalize_rows(scores)
-        return jnp.dot(weights, value_rows, preferred_element_type=jnp.float32).astype(jnp.bfloat16)
-
-    starts = jnp.arange(total // block_rows, dtype=jnp.int32) * block_rows
-    return lax.map(tagged_one_block, starts).reshape(total, HD)
-
-
-def pooled_tasks(pool_rows, pool_counts):
-    sources, pool_size = (pool_rows.shape[0], pool_rows.shape[1])
+        highest = jnp.max(scores, axis=-1, keepdims=True)
+        raised = jnp.exp2((scores - highest) * exponent_scale)
+        inverse = 1.0 / jnp.sum(raised, axis=-1, keepdims=True)
+        weights = (raised * inverse).astype(jnp.bfloat16)
+        mixed[pl.ds(start, BLOCK), :] = jnp.dot(
+            weights, values[pl.ds(key_start, CSIZE), :], preferred_element_type=jnp.float32
+        )
+
+
+def query_part(sources, stride, width, task_slots, run, counts_ref, query_ref, keys, values, out_ref, flat, packed, mixed, spread):
+    flat[pl.ds(0, sources * stride), :] = query_ref[...].astype(jnp.float32)
+    packed[...] = jnp.zeros_like(packed)
+    mixed[...] = jnp.zeros_like(mixed)
+    spread[...] = jnp.zeros_like(spread)
+    firsts = []
+    place = jnp.int32(0)
+    for task in range(task_slots):
+        firsts.append(place)
+
+        def pack(source, place, task=task):
+            first = source * stride
+            for earlier in range(task):
+                first = first + counts_ref[source * task_slots + earlier]
+            packed[pl.ds(place, run), :] = flat[pl.ds(first, run), :]
+            return place + counts_ref[source * task_slots + task]
+
+        end = lax.fori_loop(0, sources, pack, place)
+        place = (end + BLOCK - 1) // BLOCK * BLOCK
+    bounds = firsts + [place]
+    for task in range(task_slots):
+        attend(packed, keys, values, mixed, bounds[task], bounds[task + 1], task * CSIZE)
+
+    def unpack(source, places):
+        after = []
+        first = source * width
+        for task in range(task_slots):
+            count = counts_ref[source * task_slots + task]
+            spread[pl.ds(first, run), :] = mixed[pl.ds(places[task], run), :]
+            first = first + count
+            after.append(places[task] + count)
+        return tuple(after)
+
+    lax.fori_loop(0, sources, unpack, tuple(firsts))
+    out_ref[...] = spread[pl.ds(0, sources * width), :].astype(jnp.bfloat16)
+
+
+def first_kernel(sources, pool_size, stride, width, task_slots, run, query_run, counts_ref, part_ref, pair_ref, query_ref, out_ref, keys_ref, values_ref, wide_k, wide_v, tight_k, tight_v, flat, packed, mixed, spread):
+    total = sources * pool_size
+    chunk = total // 8
+
+    @pl.loop(0, 8)
+    def _(step):
+        start = pl.multiple_of(step * chunk, chunk)
+        wide_k[pl.ds(start, chunk), :] = pair_ref[pl.ds(start, chunk), :HD].astype(jnp.float32)
+        wide_v[pl.ds(start, chunk), :] = pair_ref[pl.ds(start, chunk), HD:].astype(jnp.float32)
+
+    for task in range(task_slots):
+
+        def pack(source, place, task=task):
+            first = source * pool_size
+            for earlier in range(task):
+                first = first + counts_ref[source * task_slots + earlier]
+            tight_k[pl.ds(place, run), :] = wide_k[pl.ds(first, run), :]
+            tight_v[pl.ds(place, run), :] = wide_v[pl.ds(first, run), :]
+            return place + counts_ref[source * task_slots + task]
+
+        lax.fori_loop(0, sources, pack, jnp.int32(task * CSIZE))
+
+    @pl.loop(0, task_slots * CSIZE // 512)
+    def _(step):
+        start = pl.multiple_of(step * 512, 512)
+        keys_ref[pl.ds(start, 512), :] = tight_k[pl.ds(start, 512), :].astype(jnp.bfloat16)
+        values_ref[pl.ds(start, 512), :] = tight_v[pl.ds(start, 512), :].astype(jnp.bfloat16)
+
+    query_part(sources, stride, width, task_slots, query_run, part_ref, query_ref, keys_ref, values_ref, out_ref, flat, packed, mixed, spread)
+
+
+def second_kernel(sources, stride, width, task_slots, query_run, part_ref, query_ref, keys_ref, values_ref, out_ref, flat, packed, mixed, spread):
+    query_part(sources, stride, width, task_slots, query_run, part_ref, query_ref, keys_ref, values_ref, out_ref, flat, packed, mixed, spread)
+
+
+def part_counts(pool_counts, low, high):
+    ends = jnp.cumsum(pool_counts, axis=1)
+    return jnp.clip(ends, low, high) - jnp.clip(ends - pool_counts, low, high)
+
+
+def query_scratch(sources, stride, width, task_slots, query_run):
+    most = sources * width + task_slots * BLOCK
+    return [
+        pltpu.VMEM((sources * stride + query_run, HD), jnp.float32),
+        pltpu.VMEM((most + query_run, HD), jnp.float32),
+        pltpu.VMEM((most + query_run, HD), jnp.float32),
+        pltpu.VMEM((sources * width + query_run, HD), jnp.float32),
+    ]
+
+
+SMEM_SPEC = pl.BlockSpec(memory_space=pltpu.SMEM)
+VMEM_SPEC = pl.BlockSpec(memory_space=pltpu.VMEM)
+
+
+def attention_cost(rows):
+    return pl.CostEstimate(
+        flops=4 * rows * CSIZE * HD * 2, bytes_accessed=rows * 8 * HD, transcendentals=rows * CSIZE
+    )
+
+
+def first_tasks(pairs, queries, pool_counts, width, run):
+    sources, pool_size = (pairs.shape[0], pairs.shape[1])
+    stride = queries.shape[1]
     task_slots = pool_counts.shape[1]
-    bounds = jnp.cumsum(pool_counts, axis=1)
-    slot_ids = jnp.arange(pool_size, dtype=jnp.int32)
-    task_of = jnp.sum(
-        (bounds[:, None, :] <= slot_ids[None, :, None]).astype(jnp.int32), axis=2
-    ).reshape(-1)
-    alive = task_of < task_slots
-    key_tags = jnp.where(alive, task_of, -1)
-    result = tagged_attention(pool_rows.reshape(-1, 3 * HD), task_of, key_tags)
-    result = jnp.where(alive[:, None], result, jnp.zeros_like(result))
-    return result.reshape(sources, pool_size, HD)
+    total, rows = (sources * pool_size, task_slots * CSIZE)
+    query_run = min(run, (width + 7) // 8 * 8)
+    exact = jax.ShapeDtypeStruct((rows, HD), jnp.bfloat16)
+    return pl.pallas_call(
+        functools.partial(first_kernel, sources, pool_size, stride, width, task_slots, run, query_run),
+        out_shape=(jax.ShapeDtypeStruct((sources * width, HD), jnp.bfloat16), exact, exact),
+        in_specs=[SMEM_SPEC, SMEM_SPEC, VMEM_SPEC, VMEM_SPEC],
+        out_specs=(VMEM_SPEC,) * 3,
+        scratch_shapes=[pltpu.VMEM((total + run, HD), jnp.float32)] * 2
+        + [pltpu.VMEM((rows + run, HD), jnp.float32)] * 2
+        + query_scratch(sources, stride, width, task_slots, query_run),
+        compiler_params=pltpu.CompilerParams(vmem_limit_bytes=56 * 1024 * 1024),
+        cost_estimate=attention_cost(sources * width),
+    )(
+        pool_counts.reshape(-1),
+        part_counts(pool_counts, 0, width).reshape(-1),
+        pairs.reshape(total, 2 * HD),
+        queries.reshape(sources * stride, HD),
+    )
+
+
+def second_tasks(queries, keys, values, pool_counts, low, run):
+    sources, width = (queries.shape[0], queries.shape[1])
+    task_slots = pool_counts.shape[1]
+    query_run = min(run, (width + 7) // 8 * 8)
+    return pl.pallas_call(
+        functools.partial(second_kernel, sources, width, width, task_slots, query_run),
+        out_shape=jax.ShapeDtypeStruct((sources * width, HD), jnp.bfloat16),
+        in_specs=[SMEM_SPEC] + [VMEM_SPEC] * 3,
+        out_specs=VMEM_SPEC,
+        scratch_shapes=query_scratch(sources, width, width, task_slots, query_run),
+        compiler_params=pltpu.CompilerParams(vmem_limit_bytes=56 * 1024 * 1024),
+        cost_estimate=attention_cost(sources * width),
+    )(
+        part_counts(pool_counts, low, low + width).reshape(-1),
+        queries.reshape(sources * width, HD),
+        keys,
+        values,
+    )
 
 
 def route_plan(assignment, cluster_count):
@@ -117,21 +248,24 @@
     return (member_int, position, per_task)
 
 
-def place_rows(slot_local, region, qkv_heads):
-    slot_ids = jnp.arange(region, dtype=jnp.int32)
-    table = (slot_ids[None, :, None] == jnp.transpose(slot_local)[:, None, :]).astype(jnp.bfloat16)
-    placed = jnp.einsum(
-        "hst,thf->hsf", table, qkv_heads, preferred_element_type=jnp.float32
-    ).astype(jnp.bfloat16)
-    return (table, placed)
-
-
-def collect_rows(table, came_back, region):
-    heads_back = came_back.reshape(HC, region, HD)
-    mixed = jnp.einsum(
-        "hst,hsf->thf", table, heads_back, preferred_element_type=jnp.float32
-    ).astype(jnp.bfloat16)
-    return mixed.reshape(mixed.shape[0], HC * HD)
+def slot_table(slot_local, groups, pool_size, low, high):
+    slot_ids = jnp.arange(groups * (high - low), dtype=jnp.int32)
+    slot_ids = slot_ids // (high - low) * pool_size + slot_ids % (high - low) + low
+    return (slot_ids[None, :, None] == jnp.transpose(slot_local)[:, None, :]).astype(jnp.bfloat16)
+
+
+def place_rows(table, rows, shards):
+    placed = jnp.einsum("hst,thf->hsf", table, rows, preferred_element_type=jnp.float32)
+    return placed.astype(jnp.bfloat16).reshape(shards, -1, rows.shape[2])
+
+
+def collect_rows(table, came_back):
+    heads_back = came_back.reshape(HC, -1, HD)
+    return jnp.einsum("hst,hsf->thf", table, heads_back, preferred_element_type=jnp.float32)
+
+
+def exchange(value):
+    return lax.all_to_all(value, ("sx", "sy"), split_axis=0, concat_axis=0, tiled=True)
 
 
 def body(activations, norm_gain, w_local, w_cluster, w_output, assignment):
@@ -158,18 +292,34 @@
     offsets = (jnp.cumsum(send_counts, axis=1) - send_counts).reshape(HC, cluster_count)
     offset_of = jnp.sum(member_int * offsets[None, :, :], axis=2)
     groups_head = cluster_count // task_slots
-    region = groups_head * pool_size
     local_group = assignment // task_slots
     slot_local = local_group * pool_size + offset_of + position
-    table, placed = place_rows(slot_local, region, qkv_heads)
-    send_pool = placed.reshape(shards, pool_size, 3 * HD)
-    got_pool, got_counts = (
-        lax.all_to_all(send_pool, ("sx", "sy"), split_axis=0, concat_axis=0, tiled=True),
-        lax.all_to_all(send_counts, ("sx", "sy"), split_axis=0, concat_axis=0, tiled=True),
-    )
-    finished = pooled_tasks(got_pool, got_counts)
-    came_back = lax.all_to_all(finished, ("sx", "sy"), split_axis=0, concat_axis=0, tiled=True)
-    cluster_mix = collect_rows(table, came_back, region)
+    split = (pool_size // 2 + 7) // 8 * 8
+    table = slot_table(slot_local, groups_head, pool_size, 0, pool_size)
+    table_first = slot_table(slot_local, groups_head, pool_size, 0, split)
+    table_second = slot_table(slot_local, groups_head, pool_size, split, pool_size)
+    got_pairs = exchange(place_rows(table, qkv_heads[:, :, HD:], shards))
+    count_rows = jnp.pad(send_counts, ((0, 0), (0, 8 - task_slots))).astype(jnp.bfloat16)
+    count_rows = jnp.broadcast_to(count_rows[:, :, None], (shards, 8, HD))
+    first_send = jnp.concatenate(
+        [place_rows(table_first, qkv_heads[:, :, :HD], shards), count_rows], axis=1
+    )
+    first_send, got_pairs = lax.optimization_barrier((first_send, got_pairs))
+    got_first = exchange(first_send)
+    second_send, local_mix, got_first = lax.optimization_barrier(
+        (place_rows(table_second, qkv_heads[:, :, :HD], shards), local_mix, got_first)
+    )
+    got_second = exchange(second_send)
+    got_counts = got_first[:, split : split + task_slots, 0].astype(jnp.int32)
+    run = (mean_rows + mean_rows // 2 + mean_rows // 4 + 7) // 8 * 8
+    done_first, keys, values = first_tasks(got_pairs, got_first, got_counts, split, run)
+    done_first, got_second = lax.optimization_barrier((done_first, got_second))
+    back_first = exchange(done_first.reshape(shards, split, HD))
+    done_second = second_tasks(got_second, keys, values, got_counts, split, run)
+    done_second, back_first = lax.optimization_barrier((done_second, back_first))
+    back_second = exchange(done_second.reshape(shards, pool_size - split, HD))
+    cluster_mix = collect_rows(table_first, back_first) + collect_rows(table_second, back_second)
+    cluster_mix = cluster_mix.astype(jnp.bfloat16).reshape(tok_rows, HC * HD)
     combined = jnp.concatenate([local_mix, cluster_mix], axis=1)
     projected = jnp.dot(combined, w_output, preferred_element_type=jnp.float32)
     return (activations.astype(jnp.float32) + projected).astype(jnp.bfloat16)

time: 311 us -> 211 us (0.68)
  matrix products: 103 us -> 40.2 us
  loops' own time: 32.7 us -> 0 us
  waiting for transfers between devices: 90.2 us -> 58 us
  Pallas kernels: 0 us -> 29 us
  starting transfers between devices: 21.8 us -> 49.1 us
  local copies, waits for them, and re-layouts: 25.9 us -> 8.93 us
  other arithmetic: 35.1 us -> 24.6 us
    dot_general x33 -> x3, matrix products: 77 us -> 6.29 us  [place_rows(): jnp.einsum('hst,thf->hsf', table, rows, preferred_element_type=jnp.float32)]
    another operation x1 -> x0, loops' own time: 32.7 us -> none  [tagged_attention(): return lax.map(tagged_one_block, starts).reshape(total, HD)]
    all_to_all x3 -> x5, waiting for transfers between devices: 90.2 us -> 58 us  [exchange(): lax.all_to_all(value, ('sx', 'sy'), split_axis=0, concat_axis=0, tiled=True)]
    pallas_call x0 -> x2, Pallas kernels: none -> 29 us  [the longest x1 18 us: first_tasks(): pl.pallas_call(functools.partial(first_kernel, sources, pool_size, stride...]
    all_to_all x3 -> x5, starting transfers between devices: 18.7 us -> 46 us  [exchange(): lax.all_to_all(value, ('sx', 'sy'), split_axis=0, concat_axis=0, tiled=True)]
    reduce_sum x17 -> x0, other arithmetic: 16.7 us -> none  [the longest x16 16.7 us: normalize_rows(): jnp.sum(raised, axis=-1, keepdims=True)]
    dynamic_slice x32 -> x0, local copies, waits for them, and re-layouts: 11.7 us -> none  [the longest x16 10.5 us: tagged_attention(): return lax.map(tagged_one_block, starts).reshape(total, HD)]
    sub x1, other arithmetic: 5.97 us -> 13.1 us  [normalize_rows(): raised = jnp.exp(scores - highest)]
  transfers between devices with their start and end apart: 4 -> 6, of which waited for: 2 -> 3; matrix products, arithmetic and copies ran while one was open for 49% -> 23% of each run, Pallas kernels for 0% -> 14%
where the time goes in v2:
time: 211 us; the launch traced here: 210 us
  waiting for transfers between devices  58 us (27%)
  starting transfers between devices  49.1 us (23%)
  matrix products  40.2 us (19%)
  Pallas kernels  29 us (14%)
  other arithmetic  24.6 us (12%)
  local copies, waits for them, and re-layouts  8.93 us (4%)
    all_to_all x5, waiting for transfers between devices, exchange(): lax.all_to_all(value, ('sx', 'sy'), split_axis=0, concat_axis=0, tiled=True)  58 us
    all_to_all x5, starting transfers between devices, exchange(): lax.all_to_all(value, ('sx', 'sy'), split_axis=0, concat_axis=0, tiled=True)  46 us
    pallas_call x1, Pallas kernels, first_tasks(): pl.pallas_call(functools.partial(first_kernel, sources, pool_size, stride...  18 us
    sub x1, other arithmetic, normalize_rows(): raised = jnp.exp(scores - highest)  13.1 us
    pallas_call x1, Pallas kernels, second_tasks(): pl.pallas_call(functools.partial(second_kernel, sources, width, width, ta...  11 us
    dot_general x2, matrix products, collect_rows(): jnp.einsum('hst,hsf->thf', table, heads_back, preferred_element_type=jnp....  6.73 us
    dot_general x1, matrix products, body(): jnp.dot(normed, w_cluster, preferred_element_type=jnp.float32)  6.64 us
    dot_general x3, matrix products, place_rows(): jnp.einsum('hst,thf->hsf', table, rows, preferred_element_type=jnp.float32)  6.29 us
  transfers between devices with their start and end apart: 6, of which 3 were waited for; matrix products, arithmetic and copies ran while one was open for 23% of the time, Pallas kernels for 14%

profile of v2, /device:TPU:0, one launch (start us, length us, event | category | flops | bytes accessed | tf_op | source)
XLA Modules:
  0.0 210.2 jit_solution(9537445371690203231)
XLA Ops:
  0.0 0.0 copy-start
  0.0 1.7 fusion.26
  1.7 0.9 convert_reduce_fusion
  2.6 0.1 reshape_reshape.3
  2.7 0.2 reduce_window_sum.22
  2.9 0.1 reduce_window_sum.23
  2.9 0.8 select_reduce_fusion
  3.8 0.1 eq.72
  3.9 1.1 fusion.53
  4.9 6.6 %convolution_convert_fusion = bf16[512,3072]{1,0:T(8,128)(2,1)S(1)} fusion(bf16[1024,3072]{1,0:T(8,128)(2,1)} %param.9, bf16[512,1024]{1,0:T(8,128)(2,1)} %param.6, f32[1024]{0:T(1024)} %param.7, f32[512]{0:T(512)S(1)} %add_rsqrt_fusion), kind=kOutput, calls=%fused_computation.17 | convolution fusion | flops 3224895488 | bytes 10491904 | tf_op jit(solution)/shard_map/dot_general | solution.py:283
  11.6 0.7 copy.37
  12.3 0.0 copy-start.1
  12.3 0.0 copy-start.4
  12.4 0.1 slice.37
  12.5 1.5 copy-done.1
  14.0 0.0 copy-done.4
  14.0 3.4 %fusion.33 = bf16[8,640,256]{2,1,0:T(8,128)(2,1)} fusion(bf16[512,8,256]{2,1,0:T(8,128)(2,1)S(1)} %slice.37, s32[8,512]{1,0:T(8,128)S(1)} %fusion.75, s32[640]{0:T(1024)S(1)} %fusion.84), kind=kOutput, calls=%fused_computation.46 | convolution fusion | flops 1346109440 | bytes 4737536 | tf_op jit(solution)/shard_map/hst,thf->hsf/dot_general | solution.py:258
  17.5 0.0 copy-start.6
  17.5 7.4 %all-to-all-start = ((bf16[32,160,256]{2,1,0:T(8,128)(2,1)}), bf16[32,160,256]{2,1,0:T(8,128)(2,1)}, u32[]{:S(2)}, u32[]{:S(2)}) async-start(bf16[32,160,256]{2,1,0:T(8,128)(2,1)} %bitcast.56), calls=%async_computation | async-start | bytes 5242880 | tf_op jit(solution)/shard_map/all_to_all | solution.py:268
  24.9 0.0 copy-done
  24.9 0.0 copy-done.6
  24.9 3.1 %convolution_convert_fusion.1 = bf16[512,1536]{1,0:T(8,128)(2,1)S(1)} fusion(bf16[1024,1536]{1,0:T(8,128)(2,1)S(1)} %copy-done, bf16[512,1024]{1,0:T(8,128)(2,1)} %param.6, f32[1024]{0:T(1024)S(1)} %copy-done.6, f32[512]{0:T(512)S(1)} %add_rsqrt_fusion), kind=kOutput, calls=%fused_computation.25 | convolution fusion | flops 1613496320 | bytes 5773312 | tf_op jit(solution)/shard_map/dot_general | solution.py:282
  28.1 0.0 copy-start.2
  28.1 1.1 copy-done.2
  29.2 1.1 slice.33
  30.3 3.1 %collective-permute-start = (bf16[512,1024]{1,0:T(8,128)(2,1)}, bf16[512,1024]{1,0:T(8,128)(2,1)}, u32[]{:S(2)}, u32[]{:S(2)}) collective-permute-start(bf16[512,1024]{1,0:T(8,128)(2,1)} %slice.33), channel_id=1, source_target_pairs={{0,1},{1,2},{2,3},{3,4},{4,5},{5,6},{6,7},{7,8},{8,9},{9,10},{10,1... | collective-permute-start | bytes 3145736 | tf_op jit(solution)/shard_map/ppermute | solution.py:24
  33.5 1.3 slice.32
  34.8 1.0 fusion.49
  35.8 0.1 broadcast_in_dim.38
  35.9 0.9 pad_maximum_fusion.1
  36.9 1.3 fusion.32
  38.1 1.9 fusion.46
  40.0 0.0 collective-permute-done
  40.0 2.7 %fusion.58 = (bf16[128,4,8,128]{3,2,1,0:T(8,128)(2,1)S(1)}, bf16[1024,512]{1,0:T(8,128)(2,1)}) fusion(bf16[512,1024]{1,0:T(8,128)(2,1)} %slice.33, bf16[512,1024]{1,0:T(8,128)(2,1)} %collective-permute-done), kind=kLoop, calls=%fused_computation.61 | loop fusion | flops 4194304 | bytes 4194304
  42.7 5.5 %fusion.55 = f32[4,512,1024]{2,1,0:T(8,128)} fusion(bf16[128,4,8,128]{3,2,1,0:T(8,128)(2,1)S(1)} %get-tuple-element.44, bf16[512,1536]{1,0:T(8,128)(2,1)} %copy-done.2), kind=kOutput, calls=%fused_computation.57 | convolution fusion | flops 536870912 | bytes 9961472 | tf_op jit(solution)/shard_map/while/body/eval_jaxpr/qhd,khd->hqk/dot_general | solution.py:51
  48.2 36.7 %all-to-all-done = bf16[32,160,256]{2,1,0:T(8,128)(2,1)} async-done(((bf16[32,160,256]{2,1,0:T(8,128)(2,1)}), bf16[32,160,256]{2,1,0:T(8,128)(2,1)}, u32[]{:S(2)}, u32[]{:S(2)}) %all-to-all-start) | async-done | bytes 2621472 | tf_op jit(solution)/shard_map/all_to_all | solution.py:268
  84.9 23.2 %all-to-all-start.1 = ((bf16[32,88,128]{2,1,0:T(8,128)(2,1)}), bf16[32,88,128]{2,1,0:T(8,128)(2,1)}, u32[]{:S(2)}, u32[]{:S(2)}) async-start(bf16[32,88,128]{2,1,0:T(8,128)(2,1)} %pad_maximum_fusion.1), calls=%async_computation.1 | async-start | bytes 1441792 | tf_op jit(solution)/shard_map/all_to_all | solution.py:268
  108.2 13.1 %fusion.99 = (f32[4,512]{1,0:T(4,128)S(1)}, f32[4,512,1024]{2,1,0:T(8,128)}) fusion(f32[4,512,1024]{2,1,0:T(8,128)} %fusion.55, pred[512,1024]{1,0:T(8,128)(4,1)} %fusion.32), kind=kOutput, calls=%fused_computation.125 | output fusion | flops 12583935 | bytes 17309696 | tf_op jit(solution)/shard_map/while/body/eval_jaxpr/sub | solution.py:35
  121.3 2.3 %copy.32 = bf16[1024,512]{0,1:T(8,128)(2,1)} copy(bf16[1024,512]{1,0:T(8,128)(2,1)} %get-tuple-element.45) | data formatting | bytes 2097152 | tf_op jit(solution)/shard_map/while/body/eval_jaxpr/reshape | solution.py:49
  123.6 6.1 %fusion.52 = bf16[4,128,512]{2,1,0:T(8,128)(2,1)} fusion(bf16[1024,4,128]{0,2,1:T(8,128)(2,1)} %bitcast.58, f32[4,512,1024]{2,1,0:T(8,128)} %get-tuple-element.49, f32[4,512]{1,0:T(4,128)S(1)} %get-tuple-element.48), kind=kOutput, calls=%fused_computation.53 | convolution fusion | flops 541327360 | bytes 9969664 | tf_op jit(solution)/shard_map/while/body/eval_jaxpr/hqk,khd->qhd/dot_general | solution.py:63
  129.7 0.0 all-to-all-done.1
  129.7 5.9 %all-to-all-start.2 = ((bf16[32,80,128]{2,1,0:T(8,128)(2,1)}), bf16[32,80,128]{2,1,0:T(8,128)(2,1)}, u32[]{:S(2)}, u32[]{:S(2)}) async-start(bf16[32,80,128]{2,1,0:T(8,128)(2,1)} %bitcast.59), calls=%async_computation.2 | async-start | bytes 1310720 | tf_op jit(solution)/shard_map/all_to_all | solution.py:268
  135.6 1.5 fusion.95
  137.0 0.1 reshape.212.counts_ref
  137.2 0.0 copy-start.5
  137.2 0.9 slice_convert_fusion
  138.0 0.1 copy.30
  138.2 0.1 copy.31
  138.2 0.1 reduce_window_sum.25
  138.4 0.5 clamp_subtract_fusion
  138.9 0.0 copy-done.5
  138.9 18.0 %shard_map.64 = (bf16[2560,128]{1,0:T(8,128)(2,1)}, bf16[4096,128]{1,0:T(8,128)(2,1)}, bf16[4096,128]{1,0:T(8,128)(2,1)}) custom-call(s32[64]{0:T(128)} %copy-done.5, s32[64]{0:T(128)} %get-tuple-element.46.part_ref, bf16[5120,256]{1,0:T(8,128)(2,1)} %bitcast.12.pair_ref, bf16[2816,128]{1,0:T(8,128)(2,1)} %bitcast.13.query_ref), custom_call_target="tpu_custom_call" | custom-call | flops 5368709120 | bytes 2621440 | tf_op jit(solution)/shard_map/pallas_call | solution.py:198
  156.9 0.0 all-to-all-done.2
  156.9 5.9 %all-to-all-start.3 = ((bf16[32,80,128]{2,1,0:T(8,128)(2,1)}), bf16[32,80,128]{2,1,0:T(8,128)(2,1)}, u32[]{:S(2)}, u32[]{:S(2)}) async-start(bf16[32,80,128]{2,1,0:T(8,128)(2,1)} %bitcast.60), calls=%async_computation.3 | async-start | bytes 1310720 | tf_op jit(solution)/shard_map/all_to_all | solution.py:268
  162.8 11.0 %shard_map.65 = bf16[2560,128]{1,0:T(8,128)(2,1)} custom-call(s32[64]{0:T(128)} %get-tuple-element.47.part_ref, bf16[2560,128]{1,0:T(8,128)(2,1)} %bitcast.14.query_ref, bf16[4096,128]{1,0:T(8,128)(2,1)} %get-tuple-element.39.keys_ref, bf16[4096,128]{1,0:T(8,128)(2,1)} %get-tuple-element.40.values_ref), custom_call_target="tpu_custom_call" | custom-call | flops 5368709120 | bytes 2621440 | tf_op jit(solution)/shard_map/pallas_call | solution.py:220
  173.8 6.9 %all-to-all-done.3 = bf16[32,80,128]{2,1,0:T(8,128)(2,1)} async-done(((bf16[32,80,128]{2,1,0:T(8,128)(2,1)}), bf16[32,80,128]{2,1,0:T(8,128)(2,1)}, u32[]{:S(2)}, u32[]{:S(2)}) %all-to-all-start.3) | async-done | bytes 655392 | tf_op jit(solution)/shard_map/all_to_all | solution.py:268
  180.8 3.5 %all-to-all-start.4 = ((bf16[32,80,128]{2,1,0:T(8,128)(2,1)}), bf16[32,80,128]{2,1,0:T(8,128)(2,1)}, u32[]{:S(2)}, u32[]{:S(2)}) async-start(bf16[32,80,128]{2,1,0:T(8,128)(2,1)} %bitcast.61), calls=%async_computation.4 | async-start | bytes 1310720 | tf_op jit(solution)/shard_map/all_to_all | solution.py:268
  184.3 3.6 %fusion.3 = f32[8,128,512]{2,1,0:T(8,128)} fusion(bf16[8,320,128]{2,1,0:T(8,128)(2,1)} %bitcast.16, s32[8,512]{1,0:T(8,128)S(1)} %fusion.75, s32[320]{0:T(512)S(1)} %fusion.91), kind=kOutput, calls=%fused_computation.6 | convolution fusion | flops 336855040 | bytes 2770176 | tf_op jit(solution)/shard_map/hst,hsf->thf/dot_general | solution.py:264
  187.9 14.4 %all-to-all-done.4 = bf16[32,80,128]{2,1,0:T(8,128)(2,1)} async-done(((bf16[32,80,128]{2,1,0:T(8,128)(2,1)}), bf16[32,80,128]{2,1,0:T(8,128)(2,1)}, u32[]{:S(2)}, u32[]{:S(2)}) %all-to-all-start.4) | async-done | bytes 655392 | tf_op jit(solution)/shard_map/all_to_all | solution.py:268
  202.3 0.0 copy-start.3
  202.3 3.1 %add_convert_fusion = bf16[8,128,512]{2,1,0:T(8,128)(2,1)S(1)} fusion(f32[8,128,512]{2,1,0:T(8,128)} %fusion.3, bf16[8,320,128]{2,1,0:T(8,128)(2,1)} %bitcast.18, s32[8,512]{1,0:T(8,128)S(1)} %fusion.75, s32[320]{0:T(512)S(1)} %broadcast_add_fusion), kind=kOutput, calls=%fused_computation.41 | convolution fusion | flops 337903616 | bytes 3818752 | tf_op jit(solution)/shard_map/hst,hsf->thf/dot_general | solution.py:264
  205.4 0.0 copy-done.3
  205.4 0.0 copy-done.7
  205.5 4.7 %fusion.29 = bf16[512,1024]{1,0:T(8,128)(2,1)} fusion(bf16[512,1024]{1,0:T(8,128)(2,1)S(1)} %copy-done.3, bf16[1536,1024]{1,0:T(8,128)(2,1)} %param.10, bf16[512,1024]{0,1:T(8,128)(2,1)S(1)} %bitcast.57, bf16[512,512]{0,1:T(8,128)(2,1)S(1)} %bitcast.64), kind=kOutput, calls=%fused_computation.37 | convolution fusion | flops 1615331328 | bytes 6815744 | tf_op jit(solution)/shard_map/dot_general | solution.py:324
  (13 shorter events, 0.1 us)
Async XLA Ops:
  0.0 24.9 %copy-start = (bf16[1024,1536]{1,0:T(8,128)(2,1)S(1)}, bf16[1024,1536]{1,0:T(8,128)(2,1)}, u32[]{:S(2)}) copy-start(bf16[1024,1536]{1,0:T(8,128)(2,1)} %param.8) | copy-start | bytes 9437188
  12.3 1.7 copy-start.1
  12.3 1.7 copy-start.4
  17.5 7.5 %copy-start.6 = (f32[1024]{0:T(1024)S(1)}, f32[1024]{0:T(1024)}, u32[]{:S(2)}) copy-start(f32[1024]{0:T(1024)} %param.7) | copy-start | bytes 12292
  17.5 67.5 %all-to-all-start = ((bf16[32,160,256]{2,1,0:T(8,128)(2,1)}), bf16[32,160,256]{2,1,0:T(8,128)(2,1)}, u32[]{:S(2)}, u32[]{:S(2)}) async-start(bf16[32,160,256]{2,1,0:T(8,128)(2,1)} %bitcast.56), calls=%async_computation | async-start | bytes 5242880 | tf_op jit(solution)/shard_map/all_to_all | solution.py:268
  28.1 1.1 copy-start.2
  30.3 9.7 %collective-permute-start = (bf16[512,1024]{1,0:T(8,128)(2,1)}, bf16[512,1024]{1,0:T(8,128)(2,1)}, u32[]{:S(2)}, u32[]{:S(2)}) collective-permute-start(bf16[512,1024]{1,0:T(8,128)(2,1)} %slice.33), channel_id=1, source_target_pairs={{0,1},{1,2},{2,3},{3,4},{4,5},{5,6},{6,7},{7,8},{8,9},{9,10},{10,1... | collective-permute-start | bytes 3145736 | tf_op jit(solution)/shard_map/ppermute | solution.py:24
  84.9 44.8 %all-to-all-start.1 = ((bf16[32,88,128]{2,1,0:T(8,128)(2,1)}), bf16[32,88,128]{2,1,0:T(8,128)(2,1)}, u32[]{:S(2)}, u32[]{:S(2)}) async-start(bf16[32,88,128]{2,1,0:T(8,128)(2,1)} %pad_maximum_fusion.1), calls=%async_computation.1 | async-start | bytes 1441792 | tf_op jit(solution)/shard_map/all_to_all | solution.py:268
  129.7 27.2 %all-to-all-start.2 = ((bf16[32,80,128]{2,1,0:T(8,128)(2,1)}), bf16[32,80,128]{2,1,0:T(8,128)(2,1)}, u32[]{:S(2)}, u32[]{:S(2)}) async-start(bf16[32,80,128]{2,1,0:T(8,128)(2,1)} %bitcast.59), calls=%async_computation.2 | async-start | bytes 1310720 | tf_op jit(solution)/shard_map/all_to_all | solution.py:268
  137.2 1.7 copy-start.5
  156.9 23.9 %all-to-all-start.3 = ((bf16[32,80,128]{2,1,0:T(8,128)(2,1)}), bf16[32,80,128]{2,1,0:T(8,128)(2,1)}, u32[]{:S(2)}, u32[]{:S(2)}) async-start(bf16[32,80,128]{2,1,0:T(8,128)(2,1)} %bitcast.60), calls=%async_computation.3 | async-start | bytes 1310720 | tf_op jit(solution)/shard_map/all_to_all | solution.py:268
  180.8 21.5 %all-to-all-start.4 = ((bf16[32,80,128]{2,1,0:T(8,128)(2,1)}), bf16[32,80,128]{2,1,0:T(8,128)(2,1)}, u32[]{:S(2)}, u32[]{:S(2)}) async-start(bf16[32,80,128]{2,1,0:T(8,128)(2,1)} %bitcast.61), calls=%async_computation.4 | async-start | bytes 1310720 | tf_op jit(solution)/shard_map/all_to_all | solution.py:268
  202.3 3.1 %copy-start.3 = (bf16[512,1024]{1,0:T(8,128)(2,1)S(1)}, bf16[512,1024]{1,0:T(8,128)(2,1)}, u32[]{:S(2)}) copy-start(bf16[512,1024]{1,0:T(8,128)(2,1)} %param.6) | copy-start | bytes 3145732
  202.3 3.2 %copy-start.7 = (bf16[4,128,512]{2,1,0:T(8,128)(2,1)S(1)}, bf16[4,128,512]{2,1,0:T(8,128)(2,1)}, u32[]{:S(2)}) copy-start(bf16[4,128,512]{2,1,0:T(8,128)(2,1)} %fusion.52) | copy-start | bytes 1572868
